TPU v7x, 256 devices: a whole 4x4x8 slice. The times are simulated.
256 devices in a mesh: hit: 16 (over z, core), head: 16 (over x, y).
Axes of the slice: x: 4, y: 4, z: 8, core: 2. Of those that a mesh axis runs over, the one named last changes fastest.
Arguments:
- slots: bfloat16 [1024, 1024], replicated, may hold values from -700 to 700
- hits: bfloat16 [131072, 1024], P(('hit', 'head')), may hold values from -15 to 15
- hit_mask: int32 [131072], P('hit'), may hold values from 0 to 1, as said below
- q_weight: bfloat16 [1024, 1024], P(None, 'head'), may hold values from -0.1875 to 0.1875
- k_weight: bfloat16 [1024, 1024], replicated, may hold values from -0.1875 to 0.1875
- v_weight: bfloat16 [1024, 1024], replicated, may hold values from -0.1875 to 0.1875
- o_weight: bfloat16 [1024, 1024], P('head'), may hold values from -0.1875 to 0.1875
Outputs:
- attended: bfloat16 [1024, 1024], P('hit', 'head')
Inputs may be any that keep to these rules, and one draw needn't show every extreme that they name: `hit_mask`: within each group of 8192 hits the real hits form a prefix of 2048 hits or more; in some group every hit is real.
All inputs are finite; a program needn't handle non-finite values.
Results may differ from a plain program's by a relative error of at most 0.0098.
Values may be sent and summed in bfloat16 or wider, within the bound.
A program may use at most 128 MiB of HBM per device.

v0:
```python
import jax
import jax.numpy as jnp
from jax import lax
from jax.sharding import PartitionSpec as P

HEAD_DIM = 64


def attend(queries_head, keys_head, values_head, valid):
    scores = jnp.dot(queries_head, keys_head.T, preferred_element_type=jnp.float32) * HEAD_DIM ** (
        -0.5
    )
    scores = jnp.where(valid[None, :] > 0, scores, jnp.float32(-1e30))
    row_top = jnp.max(scores, axis=1)
    expo = jnp.exp(scores - row_top[:, None])
    totals = jnp.sum(expo, axis=1)
    weights = expo.astype(jnp.bfloat16)
    partial_value = jnp.dot(weights, values_head, preferred_element_type=jnp.float32)
    return (row_top, totals, partial_value)


def local(slots, hits, hit_mask, q_weight, k_weight, v_weight, o_weight):
    heads_here = q_weight.shape[1] // HEAD_DIM
    slot_count = slots.shape[0]
    queries = jnp.dot(slots, q_weight, preferred_element_type=jnp.float32).astype(jnp.bfloat16)
    local_hits = hits.shape[0]
    head_devs = lax.axis_size("head")
    keys = jnp.dot(hits, k_weight, preferred_element_type=jnp.float32).astype(jnp.bfloat16)
    values = jnp.dot(hits, v_weight, preferred_element_type=jnp.float32).astype(jnp.bfloat16)
    keys = keys.reshape(local_hits, head_devs, heads_here, HEAD_DIM)
    values = values.reshape(local_hits, head_devs, heads_here, HEAD_DIM)
    both = jnp.concatenate([keys, values], axis=3)
    moved = lax.all_to_all(both, "head", split_axis=1, concat_axis=0, tiled=True)
    key_vals = moved.reshape(moved.shape[0], heads_here, 2 * HEAD_DIM)
    block = min(512, slot_count)
    block_count = slot_count // block
    queries_head = queries.reshape(block_count, block, HEAD_DIM)
    keys_head = key_vals[:, 0, :HEAD_DIM]
    values_head = key_vals[:, 0, HEAD_DIM:]

    def per_block(query_block):
        return attend(query_block, keys_head, values_head, hit_mask)

    head_top, head_sums, head_part = lax.map(per_block, queries_head)
    row_tops = [head_top.reshape(slot_count)]
    sums_list = [head_sums.reshape(slot_count)]
    partials = head_part.reshape(slot_count, HEAD_DIM)
    row_top = jnp.stack(row_tops, axis=1)
    totals = jnp.stack(sums_list, axis=1)
    overall = lax.pmax(row_top, "hit")
    scale = jnp.exp(row_top - overall)
    numer, denom = (
        lax.psum_scatter(
            partials * jnp.repeat(scale, HEAD_DIM, axis=1), "hit", scatter_dimension=0, tiled=True
        ),
        lax.psum_scatter(totals * scale, "hit", scatter_dimension=0, tiled=True),
    )
    mixed = (numer / jnp.repeat(denom, HEAD_DIM, axis=1)).astype(jnp.bfloat16)
    head_terms = jnp.dot(mixed, o_weight, preferred_element_type=jnp.float32)
    return lax.psum_scatter(head_terms, "head", scatter_dimension=1, tiled=True).astype(
        jnp.bfloat16
    )


def solution(mesh):
    placed = (P(), P(("hit", "head"), None), P("hit"), P(None, "head"), P(), P(), P("head", None))
    return jax.shard_map(
        local, mesh=mesh, in_specs=placed, out_specs=P("hit", "head"), check_vma=False
    )
```

profile of v0, /device:TPU:1, one launch (start us, length us, event | category | flops | bytes accessed | tf_op | source)
XLA Modules:
  0.0 353.4 jit_solution(13814991133026459591)
XLA Ops:
  6.5 0.0 copy-start
  6.5 1.6 copy-done
  8.1 3.5 convolution_convert_fusion
  11.6 1.5 copy.20
  13.1 4.2 %convolution_convert_fusion.1 = bf16[512,1024]{1,0:T(8,128)(2,1)} fusion(bf16[512,1024]{1,0:T(8,128)(2,1)} %param.10, bf16[1024,1024]{1,0:T(8,128)(2,1)} %param.13), kind=kOutput, calls=%fused_computation.19 | convolution fusion | flops 1074266112 | bytes 4194304 | tf_op jit(solution)/shard_map/dot_general | solution.py:28
  17.2 2.3 copy.19
  19.5 0.0 copy-start.2
  19.5 2.8 maximum_bitcast_fusion
  22.3 7.6 %all-to-all-start = ((bf16[512,16,1,128]{0,3,2,1:T(8,128)(2,1)}), bf16[512,16,1,128]{0,3,2,1:T(8,128)(2,1)}, u32[]{:S(2)}, u32[]{:S(2)}) async-start(bf16[512,16,1,128]{0,3,2,1:T(8,128)(2,1)} %maximum_bitcast_fusion), calls=%async_computation | async-start | bytes 4194304 | tf_op jit(solution)/shard_map/all_to_all | solution.py:33
  30.0 0.2 reduce-scatter.12.cloned.1.call-start
  30.2 0.0 copy-done.2
  30.2 2.3 convolution_convert_fusion.2
  32.6 0.2 copy.25
  32.8 25.4 %all-to-all-done = bf16[512,16,1,128]{0,3,2,1:T(8,128)(2,1)} async-done(((bf16[512,16,1,128]{0,3,2,1:T(8,128)(2,1)}), bf16[512,16,1,128]{0,3,2,1:T(8,128)(2,1)}, u32[]{:S(2)}, u32[]{:S(2)}) %all-to-all-start) | async-done | bytes 2097184 | tf_op jit(solution)/shard_map/all_to_all | solution.py:33
  58.2 3.9 %copy.22 = bf16[512,16,1,128]{3,0,1,2:T(8,128)(2,1)} copy(bf16[512,16,1,128]{0,3,2,1:T(8,128)(2,1)} %all-to-all-done) | data formatting | bytes 4194304 | tf_op jit(solution)/shard_map/all_to_all | solution.py:33
  62.1 0.0 copy-start.1
  62.1 4.9 %slice_bitcast_fusion = (bf16[8192,64]{1,0:T(8,128)(2,1)}, bf16[8192,64]{1,0:T(8,128)(2,1)}) fusion(bf16[8192,1,128]{2,0,1:T(8,128)(2,1)} %bitcast.63), kind=kLoop, calls=%fused_computation.15 | loop fusion | bytes 4194304 | tf_op jit(solution)/shard_map/squeeze | solution.py:39
  66.9 0.0 copy-done.1
  66.9 0.0 copy-start.3
  66.9 56.9 %while.14 = (s32[]{:T(128)}, f32[2,512]{1,0:T(2,128)S(1)}, f32[2,512]{1,0:T(2,128)S(1)}, f32[2,512,64]{1,0,2:T(2,128)S(1)}, s32[8192]{0:T(1024)S(1)}, /*index=5*...) while((s32[]{:T(128)}, f32[2,512]{1,0:T(2,128)S(1)}, ...), condition=%wide.region_3.4_spmd, body=%wide.region_0.3_spmd.sunk | while | flops 1119886336 | bytes 53297276 | solution.py:44
  66.9 8.7 %fusion.35 = (f32[512]{0:T(512)S(1)}, f32[512,8192]{1,0:T(8,128)}) fusion(pred[8192]{0:T(1024)(128)(4,1)S(1)} %broadcast_compare_fusion.2, bf16[8192,64]{1,0:T(8,128)(2,1)} %get-tuple-element.185, bf16[2,512,64]{2,1,0:T(8,128)(2,1)S(1)} %get-tuple-element.184, s32[]{:T(128)S(6)} %copy.46), kind=kOutput, calls=%fused_computation.2.clone.1 | convolution fusion | flops 549453312 | bytes 17967108 | tf_op jit(solution)/shard_map/while/body/eval_jaxpr/dot_general | solution.py:10
  75.7 9.8 %fusion.36 = f32[512]{0:T(512)S(1)} fusion(f32[512,8192]{1,0:T(8,128)} %get-tuple-element.158, f32[512]{0:T(512)S(1)} %get-tuple-element.157, pred[8192]{0:T(1024)(128)(4,1)S(1)} %broadcast_compare_fusion.2), kind=kLoop, calls=%fused_computation.4.clone.1 | loop fusion | flops 16776704 | bytes 16789504 | tf_op jit(solution)/shard_map/while/body/eval_jaxpr/reduce_sum | solution.py:16
  85.5 8.5 %fusion.37 = f32[1,512,64]{1,2,0:T(8,128)S(1)} fusion(bf16[8192,64]{1,0:T(8,128)(2,1)} %get-tuple-element.186, f32[512,8192]{1,0:T(8,128)} %get-tuple-element.158, f32[512]{0:T(512)S(1)} %get-tuple-element.157, pred[8192]{0:T(1024)(128)(4,1)S(1)} %broadcast_compare_fusion.2), kind=kOutput, calls=%fused_computation.7.clone.1 | convolution fusion | flops 553648128 | bytes 17967104 | tf_op jit(solution)/shard_map/while/body/eval_jaxpr/dot_general | solution.py:18
  94.0 0.1 copy.38
  94.1 1.2 dynamic_update_slice.16
  95.4 8.7 %fusion.35 = (f32[512]{0:T(512)S(1)}, f32[512,8192]{1,0:T(8,128)}) fusion(pred[8192]{0:T(1024)(128)(4,1)S(1)} %broadcast_compare_fusion.2, bf16[8192,64]{1,0:T(8,128)(2,1)} %get-tuple-element.185, bf16[2,512,64]{2,1,0:T(8,128)(2,1)S(1)} %get-tuple-element.184, s32[]{:T(128)S(6)} %copy.46), kind=kOutput, calls=%fused_computation.2.clone.1 | convolution fusion | flops 549453312 | bytes 17967108 | tf_op jit(solution)/shard_map/while/body/eval_jaxpr/dot_general | solution.py:10
  104.1 9.8 %fusion.36 = f32[512]{0:T(512)S(1)} fusion(f32[512,8192]{1,0:T(8,128)} %get-tuple-element.158, f32[512]{0:T(512)S(1)} %get-tuple-element.157, pred[8192]{0:T(1024)(128)(4,1)S(1)} %broadcast_compare_fusion.2), kind=kLoop, calls=%fused_computation.4.clone.1 | loop fusion | flops 16776704 | bytes 16789504 | tf_op jit(solution)/shard_map/while/body/eval_jaxpr/reduce_sum | solution.py:16
  113.9 8.5 %fusion.37 = f32[1,512,64]{1,2,0:T(8,128)S(1)} fusion(bf16[8192,64]{1,0:T(8,128)(2,1)} %get-tuple-element.186, f32[512,8192]{1,0:T(8,128)} %get-tuple-element.158, f32[512]{0:T(512)S(1)} %get-tuple-element.157, pred[8192]{0:T(1024)(128)(4,1)S(1)} %broadcast_compare_fusion.2), kind=kOutput, calls=%fused_computation.7.clone.1 | convolution fusion | flops 553648128 | bytes 17967104 | tf_op jit(solution)/shard_map/while/body/eval_jaxpr/dot_general | solution.py:18
  122.4 0.1 copy.38
  122.6 1.2 dynamic_update_slice.16
  123.9 29.2 %pmax.7 = f32[1024,1]{0,1:T(1,128)S(1)} all-reduce(f32[1024,1]{0,1:T(1,128)S(1)} %bitcast.71), channel_id=1, replica_groups=mesh['hit'=16,'head'=16] {'hit'}, use_global_device_ids=true, to_apply=%region_4.5 | all-reduce | flops 1024 | bytes 8192 | tf_op jit(solution)/shard_map/pmax | solution.py:50
  153.1 1.0 copy.28
  154.1 0.0 reduce-scatter.12.cloned.1.call-update
  154.1 0.0 reduce-scatter.10.cloned.1.call-start
  154.2 1.0 copy.26
  155.2 0.0 reduce-scatter.10.cloned.1.call-update
  155.2 0.0 reduce-scatter.14.cloned.1.call-start
  155.2 49.9 %reduce-scatter.12.cloned.1.call-done = f32[64,1]{1,0:T(8,128)} async-done(((f32[1024,1]{1,0:T(8,128)}), f32[64,1]{1,0:T(8,128)}) %reduce-scatter.12.cloned.1.call-update) | async-done | bytes 272
  205.1 0.8 copy.29
  206.0 57.6 %reduce-scatter.10.cloned.1.call-done = f32[64,64]{1,0:T(8,128)} async-done(((f32[1024,64]{1,0:T(8,128)}), f32[64,64]{1,0:T(8,128)}) %reduce-scatter.10.cloned.1.call-update) | async-done | bytes 16400
  263.6 0.8 copy.27
  264.4 0.0 copy-done.3
  264.4 1.1 convolution_bitcast_fusion
  265.5 0.0 reduce-scatter.14.cloned.1.call-update
  265.5 79.8 %reduce-scatter.14.cloned.1.call-done = f32[64,64]{1,0:T(8,128)} async-done(((f32[1024,64]{1,0:T(8,128)}), f32[64,64]{1,0:T(8,128)}) %reduce-scatter.14.cloned.1.call-update) | async-done | bytes 16400
  345.4 1.4 copy.31
  (14 shorter events, 0.3 us)
Async XLA Ops:
  6.5 1.6 copy-start
  19.5 10.7 %copy-start.2 = (bf16[1024,64]{0,1:T(8,128)(2,1)S(1)}, bf16[1024,64]{0,1:T(8,128)(2,1)}, u32[]{:S(2)}) copy-start(bf16[1024,64]{0,1:T(8,128)(2,1)} %param.12) | copy-start | bytes 393220
  22.3 35.8 %all-to-all-start = ((bf16[512,16,1,128]{0,3,2,1:T(8,128)(2,1)}), bf16[512,16,1,128]{0,3,2,1:T(8,128)(2,1)}, u32[]{:S(2)}, u32[]{:S(2)}) async-start(bf16[512,16,1,128]{0,3,2,1:T(8,128)(2,1)} %maximum_bitcast_fusion), calls=%async_computation | async-start | bytes 4194304 | tf_op jit(solution)/shard_map/all_to_all | solution.py:33
  30.0 175.2 %reduce-scatter.12.cloned.1.call-start = ((), (), s32[]{:S(2)}) async-start(), calls=%async_computation.5 | async-start | bytes 557056
  62.1 4.9 %copy-start.1 = (s32[8192]{0:T(1024)S(1)}, s32[8192]{0:T(1024)}, u32[]{:S(2)}) copy-start(s32[8192]{0:T(1024)} %param.11) | copy-start | bytes 98308
  66.9 197.5 %copy-start.3 = (bf16[64,1024]{1,0:T(8,128)(2,1)S(1)}, bf16[64,1024]{1,0:T(8,128)(2,1)}, u32[]{:S(2)}) copy-start(bf16[64,1024]{1,0:T(8,128)(2,1)} %param.15) | copy-start | bytes 393220
  154.1 109.5 %reduce-scatter.10.cloned.1.call-start = ((), (), s32[]{:S(2)}) async-start(), calls=%async_computation.4 | async-start | bytes 557056
  155.2 190.2 %reduce-scatter.14.cloned.1.call-start = ((), (), s32[]{:S(2)}) async-start(), calls=%async_computation.6 | async-start | bytes 557056
Sparse Core Ops, SparseCore 0:
  154.2 50.8 reduce-scatter.11
  207.6 55.9 reduce-scatter.9
  267.1 78.2 reduce-scatter.13
where the time goes:
time: 355 us; the launch traced here: 353 us
  waiting for transfers between devices  213 us (60%)
  matrix products  45.4 us (13%)
  blocking collectives  29.2 us (8%)
  other arithmetic  22.4 us (6%)
  local copies, waits for them, and re-layouts  22.3 us (6%)
  between operations  13.2 us (4%)
  starting transfers between devices  7.93 us (2%)
    unnamed x6, waiting for transfers between devices  187 us
    pmax x1, blocking collectives, local(): overall = lax.pmax(row_top, 'hit')  29.2 us
    all_to_all x1, waiting for transfers between devices, local(): lax.all_to_all(both, 'head', split_axis=1, concat_axis=0, tiled=True)  25.4 us
    reduce_sum x2, other arithmetic, attend(): totals = jnp.sum(expo, axis=1)  19.6 us
    dot_general x2, matrix products, attend(): jnp.dot(queries_head, keys_head.T, preferred_element_type=jnp.float32)  17.4 us
    dot_general x2, matrix products, attend(): jnp.dot(weights, values_head, preferred_element_type=jnp.float32)  17 us
    all_to_all x1, starting transfers between devices, local(): lax.all_to_all(both, 'head', split_axis=1, concat_axis=0, tiled=True)  7.62 us
  transfers between devices with their start and end apart: 4, of which 4 were waited for; matrix products, arithmetic and copies ran while one was open for 1% of the time, Pallas kernels for 0%

commit v1 on v0

v1 whole, which is shorter than its diff:
```python
import functools

import jax
import jax.numpy as jnp
from jax import lax
from jax.experimental import pallas as pl
from jax.experimental.pallas import tpu as pltpu
from jax.sharding import PartitionSpec as P

MESH = pl.DeviceIdType.MESH
HEAD_DIM = 64
SIDE = 4
F32, BF16 = jnp.float32, jnp.bfloat16
MASKED = -1e30


def kernel(
    slots_hbm, hits_hbm, mask_ref, qw_hbm, kw_hbm, vw_hbm, ow_hbm, out_ref,
    slots_v, hits_v, qw_v, wbuf, sbuf, rbuf, qt, top, acc,
    zso, zsm, zro, zrm, mt, owall,
    ld, ldk, ldv, kv_ss, kv_rs, ow_ss, ow_rs, zo_ss, zo_rs, zm_ss, zm_rs, g_ss, g_rs,
):
    i = lax.axis_index("hit")
    h = lax.axis_index("head")
    x, y = h // SIDE, h % SIDE
    yy, c = y // 2, i % 2
    other = i + 1 - 2 * c

    barrier = pltpu.get_barrier_semaphore()

    def greet_head(j, carry):
        pl.semaphore_signal(
            barrier, inc=1, device_id={"hit": i, "head": lax.rem(h + j, 16)}, device_id_type=MESH
        )
        return carry

    def greet_other(j, carry):
        pl.semaphore_signal(
            barrier, inc=1, device_id={"hit": other, "head": j}, device_id_type=MESH
        )
        return carry

    def greet_hit(j, carry):
        step = lax.rem(i + j, 16)

        @pl.when(step != other)
        def _():
            pl.semaphore_signal(
                barrier, inc=1, device_id={"hit": step, "head": h}, device_id_type=MESH
            )

        return carry

    lax.fori_loop(1, 16, greet_head, 0)
    lax.fori_loop(0, 16, greet_other, 0)
    lax.fori_loop(1, 16, greet_hit, 0)

    def offsets(t):
        u = t // 2
        return (10 - u * (u + 1) // 2) % SIDE, 1 - t % 2

    def target_pair(t):
        dx, dyy = offsets(t)
        return ((x + dx) % SIDE) * 2 + (yy + dyy) % 2

    hits_cp = pltpu.make_async_copy(hits_hbm, hits_v, ld.at[0])
    slots_cp = pltpu.make_async_copy(slots_hbm, slots_v, ld.at[1])
    qw_cp = pltpu.make_async_copy(qw_hbm, qw_v, ld.at[2])

    def weights(t):
        cols = pl.ds(pl.multiple_of(target_pair(t) * 128, 128), 128)
        return (
            pltpu.make_async_copy(kw_hbm.at[:, cols], wbuf.at[t, :, pl.ds(0, 128)], ldk.at[t]),
            pltpu.make_async_copy(vw_hbm.at[:, cols], wbuf.at[t, :, pl.ds(128, 128)], ldv.at[t]),
        )

    def start_weights(t, carry):
        for cp in weights(t):
            cp.start()
        return carry

    hits_cp.start()
    lax.fori_loop(0, 2, start_weights, 0)
    slots_cp.start()
    qw_cp.start()
    lax.fori_loop(2, 8, start_weights, 0)

    lane = lax.broadcasted_iota(jnp.int32, (512, 128), 1)
    low = lane < HEAD_DIM

    def send_kv(head):
        return pltpu.make_async_remote_copy(
            src_ref=sbuf.at[head], dst_ref=rbuf.at[h],
            send_sem=kv_ss.at[head], recv_sem=kv_rs.at[h],
            device_id={"head": head}, device_id_type=MESH,
        )

    def recv_kv(head):
        return pltpu.make_async_remote_copy(
            src_ref=sbuf.at[head], dst_ref=rbuf.at[head],
            send_sem=kv_ss.at[head], recv_sem=kv_rs.at[head],
            device_id={"head": head}, device_id_type=MESH,
        )

    hits_cp.wait()

    def project(t, carry):
        for cp in weights(t):
            cp.wait()
        both = jnp.dot(hits_v[...], wbuf[t], preferred_element_type=F32)
        keys, values = both[:, :128], both[:, 128:]
        first = jnp.where(low, keys, pltpu.roll(values, 64, 1)).astype(BF16)
        second = jnp.where(low, pltpu.roll(keys, 64, 1), values).astype(BF16)
        base = target_pair(t) * 2

        @pl.when(t == 0)
        def _():
            pl.semaphore_wait(barrier, 45)

        for j, block in ((0, first), (1, second)):
            head = base + j
            sbuf[head] = block

            @pl.when(head != h)
            def _():
                send_kv(head).start()

        return carry

    lax.fori_loop(0, 8, project, 0)

    slots_cp.wait()
    qw_cp.wait()
    queries = jnp.dot(slots_v[...], qw_v[...], preferred_element_type=F32).astype(BF16)
    queries = queries.astype(F32) * HEAD_DIM ** -0.5
    wide = jnp.concatenate([queries, jnp.zeros((1024, 64), F32)], axis=1)
    qt[...] = wide.T.astype(BF16)

    def send_ow(head):
        cols = pl.ds(pl.multiple_of((head // 2) * 128, 128), 128)
        rows = pl.ds(pl.multiple_of(h * 64, 64), 64)
        return pltpu.make_async_remote_copy(
            src_ref=ow_hbm.at[:, cols], dst_ref=owall.at[rows, :],
            send_sem=ow_ss.at[head], recv_sem=ow_rs.at[h],
            device_id={"head": head}, device_id_type=MESH,
        )

    def recv_ow(head):
        cols = pl.ds(0, 128)
        rows = pl.ds(pl.multiple_of(head * 64, 64), 64)
        return pltpu.make_async_remote_copy(
            src_ref=ow_hbm.at[:, cols], dst_ref=owall.at[rows, :],
            send_sem=ow_ss.at[head], recv_sem=ow_rs.at[head],
            device_id={"head": head}, device_id_type=MESH,
        )

    def start_ow(j, carry):
        send_ow(lax.rem(h + j, 16)).start()
        return carry

    lax.fori_loop(1, 16, start_ow, 0)
    own_cols = pl.ds(pl.multiple_of((h // 2) * 128, 128), 128)
    own_rows = pl.ds(pl.multiple_of(h * 64, 64), 64)
    own_ow = pltpu.make_async_copy(ow_hbm.at[:, own_cols], owall.at[own_rows, :], ld.at[3])
    own_ow.start()

    count = jnp.sum(mask_ref[...].astype(F32), keepdims=True)
    rowid = lax.broadcasted_iota(jnp.int32, (512, 1), 0)
    top[...] = jnp.full(top.shape, MASKED, F32)
    acc[...] = jnp.zeros(acc.shape, F32)

    def attend(kv, head):
        position = (rowid + head * 512).astype(F32)
        bias = jnp.where(position < count, 0.0, MASKED)
        vxt = jnp.where(low, jnp.ones_like(kv), kv).T
        for b in range(4):
            cols = slice(256 * b, 256 * b + 256)
            s = jnp.dot(kv, qt[:, cols], preferred_element_type=F32) + bias
            before = top[:, cols]
            now = jnp.maximum(before, jnp.max(s, axis=0, keepdims=True))
            p = jnp.exp(s - now).astype(BF16)
            acc[:, cols] = acc[:, cols] * jnp.exp(before - now) + jnp.dot(
                vxt, p, preferred_element_type=F32
            )
            top[:, cols] = now

    attend(sbuf[h], h)

    def chunk(q, carry):
        dx, dyy = offsets(q // 2)
        source = ((x + SIDE - dx) % SIDE) * SIDE + ((yy + dyy) % 2) * 2 + q % 2

        @pl.when(source != h)
        def _():
            recv_kv(source).wait_recv()
            attend(rbuf[source], source)

        return carry

    lax.fori_loop(0, 16, chunk, 0)

    for z in range(8):
        cols = slice(128 * z, 128 * z + 128)
        zso[z] = acc[64:, cols].astype(BF16)
        zsm[z, 0:1] = top[:, cols]
        zsm[z, 1:2] = acc[0:1, cols]

    def z_copy(to, src, slot):
        half = pl.ds(pl.multiple_of((src % 2) * 32, 32), 32)
        return (
            pltpu.make_async_remote_copy(
                src_ref=zso.at[src // 2, half, :], dst_ref=zro.at[slot],
                send_sem=zo_ss.at[src], recv_sem=zo_rs.at[slot],
                device_id={"hit": to}, device_id_type=MESH,
            ),
            pltpu.make_async_remote_copy(
                src_ref=zsm.at[src // 2], dst_ref=zrm.at[slot],
                send_sem=zm_ss.at[src], recv_sem=zm_rs.at[slot],
                device_id={"hit": to}, device_id_type=MESH,
            ),
        )

    def z_send(j, carry):
        to = lax.rem(i + 4 + j, 16)

        @pl.when(to != i)
        def _():
            for cp in z_copy(to, to, i):
                cp.start()

        return carry

    lax.fori_loop(0, 16, z_send, 0)
    my_half = pl.ds(pl.multiple_of(c * 32, 32), 32)
    zro[i] = zso[i // 2, my_half, :]
    zrm[i] = zsm[i // 2]

    def z_wait(j, carry):
        to = lax.rem(i + j, 16)
        for cp in z_copy(to, to, to):
            cp.wait_recv()
        return carry

    lax.fori_loop(1, 16, z_wait, 0)
    tops = zrm[:, 0:1, :]
    sums = zrm[:, 1:2, :]
    scale = jnp.exp(tops - jnp.max(tops, axis=0, keepdims=True))
    denom = jnp.sum(sums * scale, axis=0)
    numer = jnp.sum(zro[...].astype(F32) * scale, axis=0)
    mine = pl.ds(pl.multiple_of(h * 64 + c * 32, 32), 32)
    mt[mine, :] = (numer / denom).astype(BF16)

    def g_copy(hit, head, rows, s_sem, r_sem):
        return pltpu.make_async_remote_copy(
            src_ref=mt.at[rows, :], dst_ref=mt.at[rows, :],
            send_sem=g_ss.at[s_sem], recv_sem=g_rs.at[r_sem],
            device_id={"hit": hit, "head": head}, device_id_type=MESH,
        )

    me = 2 * h + c

    def g_send(j, carry):
        peer = lax.rem(me + j, 32)
        g_copy(i - c + peer % 2, peer // 2, mine, peer, me).start()
        return carry

    lax.fori_loop(1, 32, g_send, 0)

    def o_wait(j, carry):
        recv_ow(lax.rem(h + j, 16)).wait_recv()
        return carry

    lax.fori_loop(1, 16, o_wait, 0)
    own_ow.wait()

    def g_wait(j, carry):
        peer = lax.rem(me + j, 32)
        rows = pl.ds(pl.multiple_of(peer * 32, 32), 32)
        g_copy(i - c + peer % 2, peer // 2, rows, peer, peer).wait_recv()
        return carry

    lax.fori_loop(1, 32, g_wait, 0)
    full = jnp.dot(mt[...].T, owall[...], preferred_element_type=F32)
    rows_here = jnp.where(c == 0, full[:64], full[64:])
    out_ref[...] = jnp.where(h % 2 == 0, rows_here[:, :64], rows_here[:, 64:]).astype(BF16)

    def drain_head(j, carry):
        head = lax.rem(h + j, 16)
        send_kv(head).wait_send()
        send_ow(head).wait_send()
        to = lax.rem(i + j, 16)
        for cp in z_copy(to, to, to):
            cp.wait_send()
        return carry

    lax.fori_loop(1, 16, drain_head, 0)

    def drain_g(j, carry):
        peer = lax.rem(me + j, 32)
        g_copy(i - c + peer % 2, peer // 2, mine, peer, peer).wait_send()
        return carry

    lax.fori_loop(1, 32, drain_g, 0)


def local(slots, hits, hit_mask, q_weight, k_weight, v_weight, o_weight):
    anywhere = pl.BlockSpec(memory_space=pl.ANY)
    vmem = pl.BlockSpec(memory_space=pltpu.VMEM)
    dma = pltpu.SemaphoreType.DMA
    return pl.pallas_call(
        kernel,
        out_shape=jax.ShapeDtypeStruct((64, 64), BF16),
        in_specs=[anywhere, anywhere, vmem, anywhere, anywhere, anywhere, anywhere],
        out_specs=vmem,
        scratch_shapes=[
            pltpu.VMEM((1024, 1024), BF16),
            pltpu.VMEM((512, 1024), BF16),
            pltpu.VMEM((1024, 64), BF16),
            pltpu.VMEM((8, 1024, 256), BF16),
            pltpu.VMEM((16, 512, 128), BF16),
            pltpu.VMEM((16, 512, 128), BF16),
            pltpu.VMEM((128, 1024), BF16),
            pltpu.VMEM((1, 1024), F32),
            pltpu.VMEM((128, 1024), F32),
            pltpu.VMEM((8, 64, 128), BF16),
            pltpu.VMEM((8, 8, 128), F32),
            pltpu.VMEM((16, 32, 128), BF16),
            pltpu.VMEM((16, 8, 128), F32),
            pltpu.VMEM((1024, 128), BF16),
            pltpu.VMEM((1024, 128), BF16),
            dma((4,)), dma((8,)), dma((8,)),
            dma((16,)), dma((16,)), dma((16,)), dma((16,)),
            dma((16,)), dma((16,)), dma((16,)), dma((16,)),
            dma((32,)), dma((32,)),
        ],
        compiler_params=pltpu.CompilerParams(
            collective_id=0, has_side_effects=True, vmem_limit_bytes=48 << 20
        ),
    )(slots, hits, hit_mask.reshape(64, 128), q_weight, k_weight, v_weight, o_weight)


def solution(mesh):
    placed = (P(), P(("hit", "head"), None), P("hit"), P(None, "head"), P(), P(), P("head", None))
    return jax.shard_map(
        local, mesh=mesh, in_specs=placed, out_specs=P("hit", "head"), check_vma=False
    )
```

time: 355 us -> 82.2 us (0.23)
  waiting for transfers between devices: 213 us -> 0 us
  Pallas kernels: 0 us -> 74.2 us
  matrix products: 45.4 us -> 0 us
  blocking collectives: 29.2 us -> 0 us
  other arithmetic: 22.4 us -> 0 us
  local copies, waits for them, and re-layouts: 22.3 us -> 7.74 us
  between operations: 13.2 us -> 0.03 us
  starting transfers between devices: 7.93 us -> 0 us
    unnamed x6 -> x0, waiting for transfers between devices: 187 us -> none
    pallas_call x0 -> x1, Pallas kernels: none -> 74.2 us  [local(): pl.pallas_call(kernel, out_shape=jax.ShapeDtypeStruct((64, 64), BF16), in...]
    dot_general x7 -> x0, matrix products: 44.3 us -> none  [the longest x2 17.4 us: attend(): jnp.dot(queries_head, keys_head.T, preferred_element_type=jnp.float32)]
    pmax x1 -> x0, blocking collectives: 29.2 us -> none  [local(): overall = lax.pmax(row_top, 'hit')]
    all_to_all x1 -> x0, waiting for transfers between devices: 25.4 us -> none  [local(): lax.all_to_all(both, 'head', split_axis=1, concat_axis=0, tiled=True)]
    reduce_sum x2 -> x0, other arithmetic: 19.6 us -> none  [attend(): totals = jnp.sum(expo, axis=1)]
    all_to_all x1 -> x0, starting transfers between devices: 7.62 us -> none  [local(): lax.all_to_all(both, 'head', split_axis=1, concat_axis=0, tiled=True)]
    squeeze x1 -> x0, local copies, waits for them, and re-layouts: 4.85 us -> none  [local(): values_head = key_vals[:, 0, HEAD_DIM:]]
  transfers between devices with their start and end apart: 4 -> 0, of which waited for: 4 -> 0; matrix products, arithmetic and copies ran while one was open for 1% -> 0% of each run, Pallas kernels for 0% -> 0%
where the time goes in v1:
time: 82.2 us; the launch traced here: 81.9 us
  Pallas kernels  74.2 us (90%)
  local copies, waits for them, and re-layouts  7.74 us (9%)
    pallas_call x1, Pallas kernels, local(): pl.pallas_call(kernel, out_shape=jax.ShapeDtypeStruct((64, 64), BF16), in...  74.2 us
    unnamed x12, local copies, waits for them, and re-layouts  7.74 us

profile of v1, /device:TPU:1, one launch (start us, length us, event | category | flops | bytes accessed | tf_op | source)
XLA Modules:
  0.0 81.9 jit_solution(7534307335861180498)
XLA Ops:
  0.0 1.1 %copy.8.qw_hbm = bf16[1024,64]{1,0:T(8,128)(2,1)S(1)} copy(bf16[1024,64]{0,1:T(8,128)(2,1)} %param.10) | data formatting | bytes 262144 | tf_op args[3]
  1.1 0.0 copy-start
  1.1 1.6 %copy-done = bf16[1024,1024]{1,0:T(8,128)(2,1)S(1)} copy-done((bf16[1024,1024]{1,0:T(8,128)(2,1)S(1)}, bf16[1024,1024]{1,0:T(8,128)(2,1)}, u32[]{:S(2)}) %copy-start) | copy-done | bytes 2097176
  2.7 0.0 copy-start.1
  2.7 1.6 %copy-done.1 = bf16[1024,1024]{1,0:T(8,128)(2,1)S(1)} copy-done((bf16[1024,1024]{1,0:T(8,128)(2,1)S(1)}, bf16[1024,1024]{1,0:T(8,128)(2,1)}, u32[]{:S(2)}) %copy-start.1) | copy-done | bytes 2097176
  4.3 0.0 copy-start.2
  4.3 1.2 %copy-done.2 = bf16[512,1024]{1,0:T(8,128)(2,1)S(1)} copy-done((bf16[512,1024]{1,0:T(8,128)(2,1)S(1)}, bf16[512,1024]{1,0:T(8,128)(2,1)}, u32[]{:S(2)}) %copy-start.2) | copy-done | bytes 1048600
  5.5 0.0 copy-start.3
  5.5 0.9 %copy-done.3 = bf16[64,1024]{1,0:T(8,128)(2,1)S(1)} copy-done((bf16[64,1024]{1,0:T(8,128)(2,1)S(1)}, bf16[64,1024]{1,0:T(8,128)(2,1)}, u32[]{:S(2)}) %copy-start.3) | copy-done | bytes 131096
  6.4 0.0 copy-start.4
  6.4 0.8 copy-done.4
  7.2 74.2 %shard_map.73 = bf16[64,64]{1,0:T(8,128)(2,1)S(1)} custom-call(bf16[1024,1024]{1,0:T(8,128)(2,1)S(1)} %copy-done, bf16[512,1024]{1,0:T(8,128)(2,1)S(1)} %copy-done.2, s32[64,128]{1,0:T(8,128)S(1)} %bitcast.1, bf16[1024,64]{1,0:T(8,128)(2,1)S(1)} %copy.8.qw_hbm, bf16[1024,1024]{1,0:T(8,128)(2,1)S(1)} %copy-done.1, bf16[1024,1024]{1,0:T(8,128)(2,1)} %vw_hbm.1, ...), custom_call_target="tpu_custom_call" | custom-call | tf_op jit(solution)/shard_map/pallas_call | solution.py:310
  81.3 0.6 copy.10
Async XLA Ops:
  1.1 1.6 %copy-start = (bf16[1024,1024]{1,0:T(8,128)(2,1)S(1)}, bf16[1024,1024]{1,0:T(8,128)(2,1)}, u32[]{:S(2)}) copy-start(bf16[1024,1024]{1,0:T(8,128)(2,1)} %slots_hbm.1) | copy-start | bytes 6291460
  2.7 1.6 %copy-start.1 = (bf16[1024,1024]{1,0:T(8,128)(2,1)S(1)}, bf16[1024,1024]{1,0:T(8,128)(2,1)}, u32[]{:S(2)}) copy-start(bf16[1024,1024]{1,0:T(8,128)(2,1)} %kw_hbm.1) | copy-start | bytes 6291460
  4.3 1.2 %copy-start.2 = (bf16[512,1024]{1,0:T(8,128)(2,1)S(1)}, bf16[512,1024]{1,0:T(8,128)(2,1)}, u32[]{:S(2)}) copy-start(bf16[512,1024]{1,0:T(8,128)(2,1)} %hits_hbm.1) | copy-start | bytes 3145732
  5.5 0.9 %copy-start.3 = (bf16[64,1024]{1,0:T(8,128)(2,1)S(1)}, bf16[64,1024]{1,0:T(8,128)(2,1)}, u32[]{:S(2)}) copy-start(bf16[64,1024]{1,0:T(8,128)(2,1)} %ow_hbm.1) | copy-start | bytes 393220
  6.4 0.8 copy-start.4
